TPU v7x, 32 devices: a whole 2x2x4 slice. The times are simulated.
32 devices in a mesh: worker: 8 (over z, y), mp: 4 (over x, core).
Axes of the slice: x: 2, y: 2, z: 4, core: 2. Of those that a mesh axis runs over, the one named last changes fastest.
Arguments:
- gradients: bfloat16 [128, 1048576], P('worker', 'mp'), may hold values from -30 to 30
- center: float32 [1048576], P('mp'), may hold values from -6 to 6
- outside_sq: float32 [3, 128], P(None, 'worker'), may hold values from 209715.2 to 2097152
- radius: float32 [3], replicated, may hold values from 1.5 to 3
Outputs:
- new_center: float32 [1048576], P('mp')
- norms: float32 [128], P('worker')
All inputs are finite; a program needn't handle non-finite values.
Results may differ from a plain program's by a relative error of at most 0.0003.
Values sent between devices are 32-bit elements; how exact they have to be, the bound alone decides.
No kernel may reach another device: no remote copies, remote signals or barrier semaphores. Data moves between devices by JAX's collectives and lax.ppermute only.
A program may use at most 64 MiB of HBM per device.

v0:
```python
import jax
import jax.numpy as jnp
from jax import lax
from jax.sharding import PartitionSpec as P

ITERS = 3


def shards(gradients, center, outside_sq, radius):
    workers_all = gradients.shape[0] * lax.axis_size("worker")
    root_total = jnp.sqrt(jnp.float32(center.shape[0] * lax.axis_size("mp")))
    value = center
    norms = jnp.zeros((gradients.shape[0],), jnp.float32)
    for step in range(ITERS):
        diff = gradients.astype(jnp.float32) - value[None, :]
        partial_value = jnp.sum(diff * diff, axis=1)
        squared = lax.psum(partial_value, "mp") + outside_sq[step]
        norms = jnp.sqrt(squared)
        factor = jnp.minimum(jnp.float32(1.0), radius[step] * root_total / norms)
        local = jnp.sum(factor[:, None] * diff, axis=0)
        summed = lax.psum(local, "worker")
        value = value + summed / jnp.float32(workers_all)
    return (value, norms)


def solution(mesh):
    placed = (P("worker", "mp"), P("mp"), P(None, "worker"), P())
    return jax.shard_map(
        shards, mesh=mesh, in_specs=placed, out_specs=(P("mp"), P("worker")), check_vma=False
    )
```

profile of v0, /device:TPU:0, one launch (start us, length us, event | category | flops | bytes accessed | tf_op | source)
XLA Modules:
  0.0 333.9 jit_solution(5382687448233932146)
XLA Ops:
  7.2 0.0 copy-start
  7.2 0.0 copy-start.1
  7.2 0.0 copy-start.2
  7.2 0.0 all-reduce.4.cloned.1.call-start
  7.2 5.5 %fusion.10 = f32[16]{0:T(128)S(1)} fusion(bf16[16,262144]{1,0:T(8,128)(2,1)} %param.4, f32[262144]{0:T(1024)} %param.5), kind=kLoop, calls=%fused_computation.13 | loop fusion | flops 16777200 | bytes 9437248 | tf_op jit(solution)/shard_map/reduce_sum | solution.py:16
  12.8 8.4 %psum.42 = f32[16]{0:T(128)S(1)} all-reduce(f32[16]{0:T(128)S(1)} %fusion.10), channel_id=1, replica_groups=mesh['worker'=8,'mp'=4] {'mp'}, use_global_device_ids=true, to_apply=%region_1.0 | all-reduce | flops 16 | bytes 128 | tf_op jit(solution)/shard_map/psum | solution.py:17
  21.1 0.0 copy-done.1
  21.1 0.7 fusion.20
  22.5 0.0 copy-done.2
  22.5 0.0 copy-done
  22.5 14.0 %fusion.11 = f32[262144]{0:T(1024)} fusion(bf16[16,262144]{1,0:T(8,128)(2,1)} %param.4, f32[16]{0:T(128)S(1)} %fusion.17, f32[262144]{0:T(1024)S(1)} %copy-done), kind=kLoop, calls=%fused_computation.14 | loop fusion | flops 16515072 | bytes 10485824 | tf_op jit(solution)/shard_map/reduce_sum | solution.py:20
  36.5 0.0 all-reduce.4.cloned.1.call-update
  36.5 0.0 all-reduce.6.cloned.1.call-start
  37.2 78.1 %all-reduce.4.cloned.1.call-done = f32[262144]{0:T(1024)} async-done(((f32[262144]{0:T(1024)}), f32[262144]{0:T(1024)}) %all-reduce.4.cloned.1.call-update) | async-done | bytes 1048592 | tf_op jit(solution)/shard_map/psum | solution.py:21
  115.4 1.3 multiply_add_fusion.2
  116.7 5.2 %fusion.8 = f32[16]{0:T(128)S(1)} fusion(bf16[16,262144]{1,0:T(8,128)(2,1)} %param.4, f32[262144]{0:T(1024)S(1)} %multiply_add_fusion.2), kind=kLoop, calls=%fused_computation.11 | loop fusion | flops 16777200 | bytes 9437248 | tf_op jit(solution)/shard_map/reduce_sum | solution.py:16
  121.9 6.5 %psum.44 = f32[16]{0:T(128)S(1)} all-reduce(f32[16]{0:T(128)S(1)} %fusion.8), channel_id=1, replica_groups=mesh['worker'=8,'mp'=4] {'mp'}, use_global_device_ids=true, to_apply=%region_5.0 | all-reduce | flops 16 | bytes 128 | tf_op jit(solution)/shard_map/psum | solution.py:17
  128.4 14.0 %fusion.9 = f32[262144]{0:T(1024)} fusion(bf16[16,262144]{1,0:T(8,128)(2,1)} %param.4, f32[16]{0:T(128)S(1)} %fusion.18, f32[262144]{0:T(1024)S(1)} %multiply_add_fusion.2), kind=kLoop, calls=%fused_computation.12 | loop fusion | flops 16515072 | bytes 10485824 | tf_op jit(solution)/shard_map/reduce_sum | solution.py:20
  142.4 0.0 all-reduce.6.cloned.1.call-update
  142.4 0.0 all-reduce.8.cloned.1.call-start
  143.1 76.9 %all-reduce.6.cloned.1.call-done = f32[262144]{0:T(1024)} async-done(((f32[262144]{0:T(1024)}), f32[262144]{0:T(1024)}) %all-reduce.6.cloned.1.call-update) | async-done | bytes 1048592 | tf_op jit(solution)/shard_map/psum | solution.py:21
  220.0 1.3 multiply_add_fusion.1
  221.3 5.2 %fusion.6 = f32[16]{0:T(128)S(1)} fusion(bf16[16,262144]{1,0:T(8,128)(2,1)} %param.4, f32[262144]{0:T(1024)S(1)} %multiply_add_fusion.1), kind=kLoop, calls=%fused_computation.9 | loop fusion | flops 16777200 | bytes 9437248 | tf_op jit(solution)/shard_map/reduce_sum | solution.py:16
  226.5 6.5 %psum.46 = f32[16]{0:T(128)S(1)} all-reduce(f32[16]{0:T(128)S(1)} %fusion.6), channel_id=1, replica_groups=mesh['worker'=8,'mp'=4] {'mp'}, use_global_device_ids=true, to_apply=%region_9.0 | all-reduce | flops 16 | bytes 128 | tf_op jit(solution)/shard_map/psum | solution.py:17
  233.0 0.5 divide_minimum_fusion
  233.5 14.0 %fusion.7 = f32[262144]{0:T(1024)} fusion(bf16[16,262144]{1,0:T(8,128)(2,1)} %param.4, f32[16]{0:T(128)S(1)} %get-tuple-element.2, f32[262144]{0:T(1024)S(1)} %multiply_add_fusion.1), kind=kLoop, calls=%fused_computation.10 | loop fusion | flops 16515072 | bytes 10485824 | tf_op jit(solution)/shard_map/reduce_sum | solution.py:20
  247.5 0.0 all-reduce.8.cloned.1.call-update
  247.5 77.6 %all-reduce.8.cloned.1.call-done = f32[262144]{0:T(1024)} async-done(((f32[262144]{0:T(1024)}), f32[262144]{0:T(1024)}) %all-reduce.8.cloned.1.call-update) | async-done | bytes 1048592 | tf_op jit(solution)/shard_map/psum | solution.py:21
  325.1 2.3 multiply_add_fusion
  (2 shorter events, 0.0 us)
Async XLA Ops:
  7.2 15.3 %copy-start = (f32[262144]{0:T(1024)S(1)}, f32[262144]{0:T(1024)}, u32[]{:S(2)}) copy-start(f32[262144]{0:T(1024)} %param.5) | copy-start | bytes 3145732
  7.2 14.0 %copy-start.1 = (f32[3]{0:T(128)S(1)}, f32[3]{0:T(128)}, u32[]{:S(2)}) copy-start(f32[3]{0:T(128)} %param.7) | copy-start | bytes 40
  7.2 15.3 %copy-start.2 = (f32[3,16]{1,0:T(4,128)S(1)}, f32[3,16]{1,0:T(4,128)}, u32[]{:S(2)}) copy-start(f32[3,16]{1,0:T(4,128)} %param.6) | copy-start | bytes 580
  7.2 108.2 %all-reduce.4.cloned.1.call-start = ((), (), s32[]{:S(2)}) async-start(), calls=%async_computation | async-start | bytes 2097152 | tf_op jit(solution)/shard_map/psum | solution.py:21
  36.5 183.5 %all-reduce.6.cloned.1.call-start = ((), (), s32[]{:S(2)}) async-start(), calls=%async_computation.1 | async-start | bytes 2097152 | tf_op jit(solution)/shard_map/psum | solution.py:21
  142.4 182.7 %all-reduce.8.cloned.1.call-start = ((), (), s32[]{:S(2)}) async-start(), calls=%async_computation.2 | async-start | bytes 2097152 | tf_op jit(solution)/shard_map/psum | solution.py:21
Sparse Core Ops, SparseCore 0:
  36.6 78.7 all-reduce.3
  142.5 77.4 all-reduce.5
  247.6 77.4 all-reduce.7
where the time goes:
time: 334 us
  waiting for transfers between devices  233 us (70%)
  other arithmetic  63.3 us (19%)
  blocking collectives  21.4 us (6%)
  between operations  15.8 us (5%)
    psum x3, waiting for transfers between devices, shards(): summed = lax.psum(local, 'worker')  233 us
    reduce_sum x3, other arithmetic, shards(): local = jnp.sum(factor[:, None] * diff, axis=0)  41.9 us
    psum x3, blocking collectives, shards(): squared = lax.psum(partial_value, 'mp') + outside_sq[step]  21.4 us
    reduce_sum x3, other arithmetic, shards(): partial_value = jnp.sum(diff * diff, axis=1)  15.9 us
  transfers between devices with their start and end apart: 3, of which 3 were waited for; matrix products, arithmetic and copies ran while one was open for 0% of the time, Pallas kernels for 0%

commit v1 on v0

--- a/solution.py
+++ b/solution.py
@@ -18,7 +18,9 @@
         norms = jnp.sqrt(squared)
         factor = jnp.minimum(jnp.float32(1.0), radius[step] * root_total / norms)
         local = jnp.sum(factor[:, None] * diff, axis=0)
-        summed = lax.psum(local, "worker")
+        summed = local
+        for hop in (1, 2, 4):
+            summed = summed + lax.ppermute(summed, "worker", [(dev, dev ^ hop) for dev in range(8)])
         value = value + summed / jnp.float32(workers_all)
     return (value, norms)
 

time: 334 us -> 359 us (1.075)
  waiting for transfers between devices: 233 us -> 266 us
  between operations: 15.8 us -> 2.8 us
  starting transfers between devices: 0.12 us -> 12.4 us
  other arithmetic: 63.3 us -> 52.4 us
    ppermute x0 -> x9, waiting for transfers between devices: none -> 266 us  [shards(): lax.ppermute(summed, 'worker', [(dev, dev ^ hop) for dev in range(8)])]
    psum x3 -> x0, waiting for transfers between devices: 233 us -> none  [shards(): summed = lax.psum(local, 'worker')]
    ppermute x0 -> x9, starting transfers between devices: none -> 12.4 us  [shards(): lax.ppermute(summed, 'worker', [(dev, dev ^ hop) for dev in range(8)])]
    reduce_sum x3, other arithmetic: 15.9 us -> 10.2 us  [shards(): partial_value = jnp.sum(diff * diff, axis=1)]
  transfers between devices with their start and end apart: 3 -> 9, of which waited for: 3 -> 9; matrix products, arithmetic and copies ran while one was open for 0% -> 0% of each run, Pallas kernels for 0% -> 0%
where the time goes in v1:
time: 359 us; the launch traced here: 358 us
  waiting for transfers between devices  266 us (74%)
  other arithmetic  52.4 us (15%)
  blocking collectives  24.5 us (7%)
  starting transfers between devices  12.4 us (3%)
    ppermute x9, waiting for transfers between devices, shards(): lax.ppermute(summed, 'worker', [(dev, dev ^ hop) for dev in range(8)])  266 us
    reduce_sum x3, other arithmetic, shards(): local = jnp.sum(factor[:, None] * diff, axis=0)  39.3 us
    psum x3, blocking collectives, shards(): squared = lax.psum(partial_value, 'mp') + outside_sq[step]  24.5 us
    ppermute x9, starting transfers between devices, shards(): lax.ppermute(summed, 'worker', [(dev, dev ^ hop) for dev in range(8)])  12.4 us
    reduce_sum x3, other arithmetic, shards(): partial_value = jnp.sum(diff * diff, axis=1)  10.2 us
  transfers between devices with their start and end apart: 9, of which 9 were waited for; matrix products, arithmetic and copies ran while one was open for 0% of the time, Pallas kernels for 0%

profile of v1, /device:TPU:0, one launch (start us, length us, event | category | flops | bytes accessed | tf_op | source)
XLA Modules:
  0.0 358.5 jit_solution(3368263335349401771)
XLA Ops:
  0.6 0.0 copy-start
  0.6 0.0 copy-start.1
  0.7 0.0 copy-start.2
  0.7 5.5 %fusion.10 = f32[16]{0:T(128)S(1)} fusion(bf16[16,262144]{1,0:T(8,128)(2,1)} %param.4, f32[262144]{0:T(1024)} %param.5), kind=kLoop, calls=%fused_computation.13 | loop fusion | flops 16777200 | bytes 9437248 | tf_op jit(solution)/shard_map/reduce_sum | solution.py:16
  6.2 8.4 %psum.21 = f32[16]{0:T(128)S(1)} all-reduce(f32[16]{0:T(128)S(1)} %fusion.10), channel_id=1, replica_groups=mesh['worker'=8,'mp'=4] {'mp'}, use_global_device_ids=true, to_apply=%region_1.0 | all-reduce | flops 16 | bytes 128 | tf_op jit(solution)/shard_map/psum | solution.py:17
  14.6 0.0 copy-done.1
  14.6 0.7 fusion.20
  15.9 0.0 copy-done.2
  15.9 0.0 copy-done
  15.9 0.0 slice-start
  15.9 13.1 %fusion.11 = f32[262144]{0:T(1024)S(1)} fusion(bf16[16,262144]{1,0:T(8,128)(2,1)} %param.4, f32[16]{0:T(128)S(1)} %fusion.17, f32[262144]{0:T(1024)S(1)} %copy-done), kind=kLoop, calls=%fused_computation.14 | loop fusion | flops 16515072 | bytes 10485824 | tf_op jit(solution)/shard_map/reduce_sum | solution.py:20
  29.1 0.0 slice-start.1
  29.1 1.6 collective-permute-start
  30.7 22.0 %collective-permute-done = f32[262144]{0:T(1024)S(1)} collective-permute-done((f32[262144]{0:T(1024)S(1)}, f32[262144]{0:T(1024)S(1)}, u32[]{:S(2)}, u32[]{:S(2)}) %collective-permute-start) | collective-permute-done | bytes 1048608 | tf_op jit(solution)/shard_map/ppermute | solution.py:23
  52.7 0.1 add.52
  52.9 1.8 collective-permute-start.1
  54.6 21.1 %collective-permute-done.1 = f32[262144]{0:T(1024)S(1)} collective-permute-done((f32[262144]{0:T(1024)S(1)}, f32[262144]{0:T(1024)S(1)}, u32[]{:S(2)}, u32[]{:S(2)}) %collective-permute-start.1) | collective-permute-done | bytes 1048608 | tf_op jit(solution)/shard_map/ppermute | solution.py:23
  75.7 0.1 add.53
  75.8 3.2 collective-permute-start.2
  79.8 41.6 %collective-permute-done.2 = f32[262144]{0:T(1024)S(1)} collective-permute-done((f32[262144]{0:T(1024)S(1)}, f32[262144]{0:T(1024)S(1)}, u32[]{:S(2)}, u32[]{:S(2)}) %collective-permute-start.2) | collective-permute-done | bytes 1048608 | tf_op jit(solution)/shard_map/ppermute | solution.py:23
  121.4 0.2 multiply_add_fusion.2
  121.6 0.0 slice-done
  121.6 0.0 slice-done.1
  121.7 2.3 fusion.8
  124.0 8.4 %psum.22 = f32[16]{0:T(128)S(1)} all-reduce(f32[16]{0:T(128)S(1)} %fusion.8), channel_id=1, replica_groups=mesh['worker'=8,'mp'=4] {'mp'}, use_global_device_ids=true, to_apply=%region_4.0 | all-reduce | flops 16 | bytes 128 | tf_op jit(solution)/shard_map/psum | solution.py:17
  132.4 0.0 slice-start.2
  132.4 13.1 %fusion.9 = f32[262144]{0:T(1024)S(1)} fusion(bf16[16,262144]{1,0:T(8,128)(2,1)} %param.4, f32[16]{0:T(128)S(1)} %fusion.18, f32[262144]{0:T(1024)S(1)} %multiply_add_fusion.2), kind=kLoop, calls=%fused_computation.12 | loop fusion | flops 16515072 | bytes 10485824 | tf_op jit(solution)/shard_map/reduce_sum | solution.py:20
  145.6 0.0 slice-start.3
  145.6 1.1 collective-permute-start.3
  146.6 23.4 %collective-permute-done.3 = f32[262144]{0:T(1024)S(1)} collective-permute-done((f32[262144]{0:T(1024)S(1)}, f32[262144]{0:T(1024)S(1)}, u32[]{:S(2)}, u32[]{:S(2)}) %collective-permute-start.3) | collective-permute-done | bytes 1048608 | tf_op jit(solution)/shard_map/ppermute | solution.py:23
  170.1 0.1 add.57
  170.2 0.5 collective-permute-start.4
  170.7 23.2 %collective-permute-done.4 = f32[262144]{0:T(1024)S(1)} collective-permute-done((f32[262144]{0:T(1024)S(1)}, f32[262144]{0:T(1024)S(1)}, u32[]{:S(2)}, u32[]{:S(2)}) %collective-permute-start.4) | collective-permute-done | bytes 1048608 | tf_op jit(solution)/shard_map/ppermute | solution.py:23
  193.9 0.1 add.58
  194.0 1.3 collective-permute-start.5
  195.9 43.8 %collective-permute-done.5 = f32[262144]{0:T(1024)S(1)} collective-permute-done((f32[262144]{0:T(1024)S(1)}, f32[262144]{0:T(1024)S(1)}, u32[]{:S(2)}, u32[]{:S(2)}) %collective-permute-start.5) | collective-permute-done | bytes 1048608 | tf_op jit(solution)/shard_map/ppermute | solution.py:23
  239.7 0.2 multiply_add_fusion.1
  240.0 0.0 slice-done.2
  240.0 0.0 slice-done.3
  240.0 2.3 fusion.6
  242.4 7.7 %psum.23 = f32[16]{0:T(128)S(1)} all-reduce(f32[16]{0:T(128)S(1)} %fusion.6), channel_id=1, replica_groups=mesh['worker'=8,'mp'=4] {'mp'}, use_global_device_ids=true, to_apply=%region_7.0 | all-reduce | flops 16 | bytes 128 | tf_op jit(solution)/shard_map/psum | solution.py:17
  250.0 0.5 divide_minimum_fusion
  250.6 13.0 %fusion.7 = f32[262144]{0:T(1024)S(1)} fusion(bf16[16,262144]{1,0:T(8,128)(2,1)} %param.4, f32[16]{0:T(128)S(1)} %get-tuple-element.2, f32[262144]{0:T(1024)S(1)} %multiply_add_fusion.1), kind=kLoop, calls=%fused_computation.10 | loop fusion | flops 16515072 | bytes 10485824 | tf_op jit(solution)/shard_map/reduce_sum | solution.py:20
  263.6 1.1 collective-permute-start.6
  264.6 23.3 %collective-permute-done.6 = f32[262144]{0:T(1024)S(1)} collective-permute-done((f32[262144]{0:T(1024)S(1)}, f32[262144]{0:T(1024)S(1)}, u32[]{:S(2)}, u32[]{:S(2)}) %collective-permute-start.6) | collective-permute-done | bytes 1048608 | tf_op jit(solution)/shard_map/ppermute | solution.py:23
  287.9 0.1 add.62
  288.0 0.5 collective-permute-start.7
  288.5 23.0 %collective-permute-done.7 = f32[262144]{0:T(1024)S(1)} collective-permute-done((f32[262144]{0:T(1024)S(1)}, f32[262144]{0:T(1024)S(1)}, u32[]{:S(2)}, u32[]{:S(2)}) %collective-permute-start.7) | collective-permute-done | bytes 1048608 | tf_op jit(solution)/shard_map/ppermute | solution.py:23
  311.5 0.1 add.63
  311.6 1.5 collective-permute-start.8
  313.1 44.2 %collective-permute-done.8 = f32[262144]{0:T(1024)S(1)} collective-permute-done((f32[262144]{0:T(1024)S(1)}, f32[262144]{0:T(1024)S(1)}, u32[]{:S(2)}, u32[]{:S(2)}) %collective-permute-start.8) | collective-permute-done | bytes 1048608 | tf_op jit(solution)/shard_map/ppermute | solution.py:23
  357.2 1.2 multiply_add_fusion
  (4 shorter events, 0.0 us)
Async XLA Ops:
  0.6 15.3 %copy-start = (f32[262144]{0:T(1024)S(1)}, f32[262144]{0:T(1024)}, u32[]{:S(2)}) copy-start(f32[262144]{0:T(1024)} %param.5) | copy-start | bytes 3145732
  0.6 13.9 %copy-start.1 = (f32[3]{0:T(128)S(1)}, f32[3]{0:T(128)}, u32[]{:S(2)}) copy-start(f32[3]{0:T(128)} %param.7) | copy-start | bytes 40
  0.7 15.2 %copy-start.2 = (f32[3,16]{1,0:T(4,128)S(1)}, f32[3,16]{1,0:T(4,128)}, u32[]{:S(2)}) copy-start(f32[3,16]{1,0:T(4,128)} %param.6) | copy-start | bytes 580
  15.9 105.7 %slice-start = ((s8[8388608]{0:T(1024)(128)(4,1)}), s8[4194304]{0:T(1024)(128)(4,1)S(1)}, s32[]{:S(2)}) async-start(s8[8388608]{0:T(1024)(128)(4,1)} %bitcast.24), calls=%async_computation | async-start | bytes 8388608
  29.1 92.6 %slice-start.1 = ((s8[8388608]{0:T(1024)(128)(4,1)}), s8[4194304]{0:T(1024)(128)(4,1)S(1)}, s32[]{:S(2)}) async-start(s8[8388608]{0:T(1024)(128)(4,1)} %bitcast.24), calls=%async_computation.1 | async-start | bytes 8388608
  29.1 23.6 %collective-permute-start = (f32[262144]{0:T(1024)S(1)}, f32[262144]{0:T(1024)S(1)}, u32[]{:S(2)}, u32[]{:S(2)}) collective-permute-start(f32[262144]{0:T(1024)S(1)} %fusion.11), channel_id=1, source_target_pairs={{0,4},{4,0},{8,12},{12,8},{16,20},{20,16},{24,28},{28,24},{1,5},{5... | collective-permute-start | bytes 3145736 | tf_op jit(solution)/shard_map/ppermute | solution.py:23
  52.9 22.9 %collective-permute-start.1 = (f32[262144]{0:T(1024)S(1)}, f32[262144]{0:T(1024)S(1)}, u32[]{:S(2)}, u32[]{:S(2)}) collective-permute-start(f32[262144]{0:T(1024)S(1)} %add.52), channel_id=1, source_target_pairs={{0,8},{4,12},{8,0},{12,4},{16,24},{20,28},{24,16},{28,20},{1,9},{5... | collective-permute-start | bytes 3145736 | tf_op jit(solution)/shard_map/ppermute | solution.py:23
  75.8 45.5 %collective-permute-start.2 = (f32[262144]{0:T(1024)S(1)}, f32[262144]{0:T(1024)S(1)}, u32[]{:S(2)}, u32[]{:S(2)}) collective-permute-start(f32[262144]{0:T(1024)S(1)} %add.53), channel_id=1, source_target_pairs={{0,16},{4,20},{8,24},{12,28},{16,0},{20,4},{24,8},{28,12},{1,17},{... | collective-permute-start | bytes 3145736 | tf_op jit(solution)/shard_map/ppermute | solution.py:23
  132.4 107.6 %slice-start.2 = ((s8[8388608]{0:T(1024)(128)(4,1)}), s8[4194304]{0:T(1024)(128)(4,1)S(1)}, s32[]{:S(2)}) async-start(s8[8388608]{0:T(1024)(128)(4,1)} %bitcast.26), calls=%async_computation.2 | async-start | bytes 8388608
  145.6 94.4 %slice-start.3 = ((s8[8388608]{0:T(1024)(128)(4,1)}), s8[4194304]{0:T(1024)(128)(4,1)S(1)}, s32[]{:S(2)}) async-start(s8[8388608]{0:T(1024)(128)(4,1)} %bitcast.26), calls=%async_computation.3 | async-start | bytes 8388608
  145.6 24.5 %collective-permute-start.3 = (f32[262144]{0:T(1024)S(1)}, f32[262144]{0:T(1024)S(1)}, u32[]{:S(2)}, u32[]{:S(2)}) collective-permute-start(f32[262144]{0:T(1024)S(1)} %fusion.9), channel_id=1, source_target_pairs={{0,4},{4,0},{8,12},{12,8},{16,20},{20,16},{24,28},{28,24},{1,5},{5... | collective-permute-start | bytes 3145736 | tf_op jit(solution)/shard_map/ppermute | solution.py:23
  170.2 23.6 %collective-permute-start.4 = (f32[262144]{0:T(1024)S(1)}, f32[262144]{0:T(1024)S(1)}, u32[]{:S(2)}, u32[]{:S(2)}) collective-permute-start(f32[262144]{0:T(1024)S(1)} %add.57), channel_id=1, source_target_pairs={{0,8},{4,12},{8,0},{12,4},{16,24},{20,28},{24,16},{28,20},{1,9},{5... | collective-permute-start | bytes 3145736 | tf_op jit(solution)/shard_map/ppermute | solution.py:23
  194.0 45.8 %collective-permute-start.5 = (f32[262144]{0:T(1024)S(1)}, f32[262144]{0:T(1024)S(1)}, u32[]{:S(2)}, u32[]{:S(2)}) collective-permute-start(f32[262144]{0:T(1024)S(1)} %add.58), channel_id=1, source_target_pairs={{0,16},{4,20},{8,24},{12,28},{16,0},{20,4},{24,8},{28,12},{1,17},{... | collective-permute-start | bytes 3145736 | tf_op jit(solution)/shard_map/ppermute | solution.py:23
  263.6 24.3 %collective-permute-start.6 = (f32[262144]{0:T(1024)S(1)}, f32[262144]{0:T(1024)S(1)}, u32[]{:S(2)}, u32[]{:S(2)}) collective-permute-start(f32[262144]{0:T(1024)S(1)} %fusion.7), channel_id=1, source_target_pairs={{0,4},{4,0},{8,12},{12,8},{16,20},{20,16},{24,28},{28,24},{1,5},{5... | collective-permute-start | bytes 3145736 | tf_op jit(solution)/shard_map/ppermute | solution.py:23
  288.0 23.5 %collective-permute-start.7 = (f32[262144]{0:T(1024)S(1)}, f32[262144]{0:T(1024)S(1)}, u32[]{:S(2)}, u32[]{:S(2)}) collective-permute-start(f32[262144]{0:T(1024)S(1)} %add.62), channel_id=1, source_target_pairs={{0,8},{4,12},{8,0},{12,4},{16,24},{20,28},{24,16},{28,20},{1,9},{5... | collective-permute-start | bytes 3145736 | tf_op jit(solution)/shard_map/ppermute | solution.py:23
  311.6 45.6 %collective-permute-start.8 = (f32[262144]{0:T(1024)S(1)}, f32[262144]{0:T(1024)S(1)}, u32[]{:S(2)}, u32[]{:S(2)}) collective-permute-start(f32[262144]{0:T(1024)S(1)} %add.63), channel_id=1, source_target_pairs={{0,16},{4,20},{8,24},{12,28},{16,0},{20,4},{24,8},{28,12},{1,17},{... | collective-permute-start | bytes 3145736 | tf_op jit(solution)/shard_map/ppermute | solution.py:23
